TPU v7x, 256 devices: a whole 4x4x8 slice. The times are simulated.
256 devices in a mesh: wide: 32 (over z, y), narrow: 8 (over x, core).
Axes of the slice: x: 4, y: 4, z: 8, core: 2. Of those that a mesh axis runs over, the one named last changes fastest.
Arguments:
- upstream_hot: bfloat16 [524288, 512], P(('wide', 'narrow')), may hold values from -6 to 6
- upstream_warm: bfloat16 [524288, 512], P(('wide', 'narrow')), may hold values from -6 to 6
- upstream_cold: bfloat16 [524288, 512], P(('wide', 'narrow')), may hold values from -6 to 6
- saved_hot: bfloat16 [524288, 512], P(('wide', 'narrow')), may hold values from -6 to 6
- saved_warm: bfloat16 [524288, 128], P(('wide', 'narrow')), may hold values from -6 to 6
- saved_cold: bfloat16 [32, 524288], P(None, ('wide', 'narrow')), may hold values from -6 to 6
- weight_hot: bfloat16 [512, 512], replicated, may hold values from -0.25 to 0.25
- weight_warm: bfloat16 [128, 512], replicated, may hold values from -0.25 to 0.25
- weight_cold: bfloat16 [32, 512], replicated, may hold values from -0.25 to 0.25
- owner_hot: int32 [524288, 1], P(('wide', 'narrow')), may hold values from 0 to 255; in each aligned block of 2048 rows (0 to 2047, 2048 to 4095, ...) at most 16 rows name the same one
- owner_warm: int32 [524288, 1], P(('wide', 'narrow')), may hold values from 0 to 255; in each aligned block of 2048 rows (0 to 2047, 2048 to 4095, ...) at most 16 rows name the same one
- owner_cold: int32 [524288, 1], P(('wide', 'narrow')), may hold values from 0 to 255; in each aligned block of 2048 rows (0 to 2047, 2048 to 4095, ...) at most 16 rows name the same one
- local_hot: int32 [524288], P(('wide', 'narrow')), may hold values from 0 to 511
- local_warm: int32 [524288], P(('wide', 'narrow')), may hold values from 0 to 2047
- local_cold: int32 [524288], P(('wide', 'narrow')), may hold values from 0 to 4095
Outputs:
- table_hot: float32 [131072, 512], P(('wide', 'narrow'))
- table_warm: float32 [524288, 128], P(('wide', 'narrow'))
- table_cold: float32 [32, 1048576], P(None, ('wide', 'narrow'))
- mixing_hot: float32 [512, 512], replicated
- mixing_warm: float32 [128, 512], replicated
- mixing_cold: float32 [32, 512], replicated
Inputs may be any that keep to these rules, and one draw needn't show every extreme that they name: `owner_hot`: among the 2048 lookups of the most frequent bucket on one device, at most 16 have the same owner, and that many is reached. `owner_warm`: among the 2048 lookups of the middle bucket on one device, at most 16 have the same owner, and that many is reached. `owner_cold`: among the 2048 lookups of the rarest bucket on one device, at most 16 have the same owner, and that many is reached.
All inputs are finite; a program needn't handle non-finite values.
Results may differ from a plain program's by a relative error of at most 0.0029.
Values may be sent and summed in bfloat16 or wider, within the bound.
A program may use at most 128 MiB of HBM per device.

v0:
```python
import math
import jax
import jax.numpy as jnp
from jax import lax
from jax.sharding import PartitionSpec as P

W_HOT = 512
W_WARM = 128
W_COLD = 32
LOOK = 2048
ROWS_HOT = 512
ROWS_WARM = 2048
ROWS_COLD = 4096


def project(values, weight):
    return lax.dot_general(
        values, weight, (((1,), (1,)), ((), ())), preferred_element_type=jnp.float32
    )


def pack_rows(values, owners, local_rows, capacity, devices, narrow_size):
    targets = lax.iota(jnp.int32, devices)
    onehot = (owners[:, None] == targets[None, :]).astype(jnp.int32)
    position = jnp.sum(jnp.cumsum(onehot, axis=0) * onehot, axis=1) - 1
    placed = owners * capacity + position
    columns = values.shape[1]
    buffer = jnp.zeros((devices * capacity, columns), values.dtype).at[placed].set(values)
    labels = jnp.full((devices * capacity,), -1, jnp.int32).at[placed].set(local_rows)
    wide_size = devices // narrow_size
    return (
        buffer.reshape(wide_size, narrow_size, capacity * columns),
        labels.reshape(wide_size, narrow_size, capacity),
    )


def segment_rows(terms, labels, table_rows, transposed):
    block_rows = min(512, table_rows)
    flat_labels = labels.reshape(-1)

    def one_block(start):
        index_rows = start + lax.iota(jnp.int32, block_rows)
        if transposed:
            onehot = (flat_labels[:, None] == index_rows[None, :]).astype(jnp.bfloat16)
            return lax.dot_general(
                terms, onehot, (((0,), (0,)), ((), ())), preferred_element_type=jnp.float32
            )
        onehot = (index_rows[:, None] == flat_labels[None, :]).astype(jnp.bfloat16)
        return jnp.dot(onehot, terms, preferred_element_type=jnp.float32)

    starts = jnp.arange(table_rows // block_rows, dtype=jnp.int32) * block_rows
    blocks = lax.map(one_block, starts)
    if transposed:
        return jnp.transpose(blocks, (1, 0, 2)).reshape(terms.shape[1], table_rows)
    return blocks.reshape(table_rows, terms.shape[1])


def per_device(
    upstream_hot,
    upstream_warm,
    upstream_cold,
    saved_hot,
    saved_warm,
    saved_cold,
    weight_hot,
    weight_warm,
    weight_cold,
    owner_hot,
    owner_warm,
    owner_cold,
    local_hot,
    local_warm,
    local_cold,
):
    narrow_size = lax.axis_size("narrow")
    devices = lax.axis_size("wide") * narrow_size
    capacity = max(2, 2 * LOOK // devices)
    sent_hot, label_hot = pack_rows(
        project(upstream_hot, weight_hot).astype(jnp.bfloat16),
        owner_hot[:, 0],
        local_hot,
        capacity,
        devices,
        narrow_size,
    )
    sent_warm, label_warm = pack_rows(
        project(upstream_warm, weight_warm).astype(jnp.bfloat16),
        owner_warm[:, 0],
        local_warm,
        capacity,
        devices,
        narrow_size,
    )
    sent_cold, label_cold = pack_rows(
        project(upstream_cold, weight_cold).astype(jnp.bfloat16),
        owner_cold[:, 0],
        local_cold,
        capacity,
        devices,
        narrow_size,
    )
    got_hot, got_warm, got_cold, lab_hot, lab_warm, lab_cold = (
        lax.all_to_all(
            lax.all_to_all(sent_hot, "wide", split_axis=0, concat_axis=0, tiled=True),
            "narrow",
            split_axis=1,
            concat_axis=1,
            tiled=True,
        ),
        lax.all_to_all(
            lax.all_to_all(sent_warm, "wide", split_axis=0, concat_axis=0, tiled=True),
            "narrow",
            split_axis=1,
            concat_axis=1,
            tiled=True,
        ),
        lax.all_to_all(
            lax.all_to_all(sent_cold, "wide", split_axis=0, concat_axis=0, tiled=True),
            "narrow",
            split_axis=1,
            concat_axis=1,
            tiled=True,
        ),
        lax.all_to_all(
            lax.all_to_all(label_hot, "wide", split_axis=0, concat_axis=0, tiled=True),
            "narrow",
            split_axis=1,
            concat_axis=1,
            tiled=True,
        ),
        lax.all_to_all(
            lax.all_to_all(label_warm, "wide", split_axis=0, concat_axis=0, tiled=True),
            "narrow",
            split_axis=1,
            concat_axis=1,
            tiled=True,
        ),
        lax.all_to_all(
            lax.all_to_all(label_cold, "wide", split_axis=0, concat_axis=0, tiled=True),
            "narrow",
            split_axis=1,
            concat_axis=1,
            tiled=True,
        ),
    )
    term_hot = got_hot.reshape(-1, W_HOT)
    term_warm = got_warm.reshape(-1, W_WARM)
    term_cold = got_cold.reshape(-1, W_COLD)
    table_hot = segment_rows(term_hot, lab_hot, ROWS_HOT, False)
    table_warm = segment_rows(term_warm, lab_warm, ROWS_WARM, False)
    table_cold = segment_rows(term_cold, lab_cold, ROWS_COLD, True)
    part_hot = lax.dot_general(
        saved_hot, upstream_hot, (((0,), (0,)), ((), ())), preferred_element_type=jnp.float32
    )
    part_warm = lax.dot_general(
        saved_warm, upstream_warm, (((0,), (0,)), ((), ())), preferred_element_type=jnp.float32
    )
    part_cold = jnp.dot(saved_cold, upstream_cold, preferred_element_type=jnp.float32)
    factor = 1.0 / math.sqrt(LOOK * devices)
    total_hot, total_warm, total_cold = lax.psum(
        (part_hot, part_warm, part_cold), ("wide", "narrow")
    )
    return (
        table_hot,
        table_warm,
        table_cold,
        total_hot * factor,
        total_warm * factor,
        total_cold * factor,
    )


def solution(mesh):
    placed = (
        P(("wide", "narrow"), None),
        P(("wide", "narrow"), None),
        P(("wide", "narrow"), None),
        P(("wide", "narrow"), None),
        P(("wide", "narrow"), None),
        P(None, ("wide", "narrow")),
        P(),
        P(),
        P(),
        P(("wide", "narrow"), None),
        P(("wide", "narrow"), None),
        P(("wide", "narrow"), None),
        P(("wide", "narrow")),
        P(("wide", "narrow")),
        P(("wide", "narrow")),
    )
    return jax.shard_map(
        per_device,
        mesh=mesh,
        in_specs=placed,
        out_specs=(
            P(("wide", "narrow"), None),
            P(("wide", "narrow"), None),
            P(None, ("wide", "narrow")),
            P(),
            P(),
            P(),
        ),
        check_vma=False,
    )
```

profile of v0, /device:TPU:1, one launch (start us, length us, event | category | flops | bytes accessed | tf_op | source)
XLA Modules:
  0.0 585.1 jit_solution(10837068983426819529)
XLA Ops:
  14.5 8.2 %scatter_custom_fusion = s32[4096]{0:T(1024)S(1)} fusion(s32[2048]{0:T(1024)S(1)} %bitcast.108, s32[2048]{0:T(1024)} %param.31, s32[]{:T(128)} %constant.28.clone.1), kind=kCustom, calls=%fused_computation.69 | custom fusion | bytes 16896 | tf_op jit(solution)/shard_map/scatter | solution.py:29
  23.5 12.0 %all-to-all-start = ((s32[32,1,128]{2,1,0:T(1,128)}), s32[32,1,128]{2,1,0:T(1,128)S(1)}, u32[]{:S(2)}, u32[]{:S(2)}) async-start(s32[32,1,128]{2,1,0:T(1,128)} %reshape.208), calls=%async_computation | async-start | bytes 32768 | tf_op jit(solution)/shard_map/all_to_all | solution.py:125
  47.3 8.2 %scatter_custom_fusion.2 = s32[4096]{0:T(1024)S(1)} fusion(s32[2048]{0:T(1024)S(1)} %bitcast.110, s32[2048]{0:T(1024)} %param.32, s32[]{:T(128)} %constant.28.clone.1), kind=kCustom, calls=%fused_computation.67 | custom fusion | bytes 16896 | tf_op jit(solution)/shard_map/scatter | solution.py:29
  56.3 9.2 %all-to-all-start.4 = ((s32[32,1,128]{2,1,0:T(1,128)}), s32[32,1,128]{2,1,0:T(1,128)S(1)}, u32[]{:S(2)}, u32[]{:S(2)}) async-start(s32[32,1,128]{2,1,0:T(1,128)} %reshape.212), calls=%async_computation.4 | async-start | bytes 32768 | tf_op jit(solution)/shard_map/all_to_all | solution.py:132
  65.6 8.2 %scatter_custom_fusion.4 = s32[4096]{0:T(1024)S(1)} fusion(s32[2048]{0:T(1024)S(1)} %bitcast.112, s32[2048]{0:T(1024)} %param.33, s32[]{:T(128)} %constant.28.clone.1), kind=kCustom, calls=%fused_computation.65 | custom fusion | bytes 16896 | tf_op jit(solution)/shard_map/scatter | solution.py:29
  74.6 9.2 %all-to-all-start.8 = ((s32[32,1,128]{2,1,0:T(1,128)}), s32[32,1,128]{2,1,0:T(1,128)S(1)}, u32[]{:S(2)}, u32[]{:S(2)}) async-start(s32[32,1,128]{2,1,0:T(1,128)} %reshape.216), calls=%async_computation.8 | async-start | bytes 32768 | tf_op jit(solution)/shard_map/all_to_all | solution.py:139
  86.0 6.4 %all-to-all-done.8 = s32[32,1,128]{2,1,0:T(1,128)S(1)} async-done(((s32[32,1,128]{2,1,0:T(1,128)}), s32[32,1,128]{2,1,0:T(1,128)S(1)}, u32[]{:S(2)}, u32[]{:S(2)}) %all-to-all-start.8) | async-done | bytes 16416 | tf_op jit(solution)/shard_map/all_to_all | solution.py:139
  92.4 7.5 %all-to-all-start.1 = ((s32[8,1,512]{2,1,0:T(1,128)}), s32[8,1,512]{2,1,0:T(1,128)S(1)}, u32[]{:S(2)}, u32[]{:S(2)}) async-start(s32[8,1,512]{2,1,0:T(1,128)} %reshape.210), calls=%async_computation.1 | async-start | bytes 32768 | tf_op jit(solution)/shard_map/all_to_all | solution.py:124
  111.9 6.4 %scatter_custom_fusion.5 = bf16[4096,32]{1,0:T(8,128)(2,1)S(1)} fusion(s32[2048]{0:T(1024)S(1)} %bitcast.113, bf16[2048,32]{1,0:T(8,128)(2,1)} %copy.64, bf16[]{:T(256)} %constant.37.clone.1), kind=kCustom, calls=%fused_computation.53 | custom fusion | bytes 262656 | tf_op jit(solution)/shard_map/scatter | solution.py:28
  125.4 10.5 %all-to-all-done.10 = bf16[32,8,512]{2,1,0:T(8,128)(2,1)S(1)} async-done(((bf16[32,8,512]{2,1,0:T(8,128)(2,1)}), bf16[32,8,512]{2,1,0:T(8,128)(2,1)S(1)}, u32[]{:S(2)}, u32[]{:S(2)}) %all-to-all-start.10) | async-done | bytes 262176 | tf_op jit(solution)/shard_map/all_to_all | solution.py:118
  136.0 6.2 %all-to-all-start.9 = ((s32[8,1,512]{2,1,0:T(1,128)}), s32[8,1,512]{2,1,0:T(1,128)S(1)}, u32[]{:S(2)}, u32[]{:S(2)}) async-start(s32[8,1,512]{2,1,0:T(1,128)} %reshape.218), calls=%async_computation.9 | async-start | bytes 32768 | tf_op jit(solution)/shard_map/all_to_all | solution.py:138
  154.6 6.4 %scatter_custom_fusion.3 = bf16[4096,128]{1,0:T(8,128)(2,1)S(1)} fusion(s32[2048]{0:T(1024)} %bitcast.111, bf16[2048,128]{1,0:T(8,128)(2,1)} %convolution_convert_fusion.1, bf16[]{:T(256)} %constant.37.clone.1), kind=kCustom, calls=%fused_computation.55 | custom fusion | bytes 1049088 | tf_op jit(solution)/shard_map/scatter | solution.py:28
  170.0 12.6 %scatter_custom_fusion.1 = bf16[4096,512]{1,0:T(8,128)(2,1)} fusion(s32[2048]{0:T(1024)} %bitcast.109, bf16[2048,512]{1,0:T(8,128)(2,1)} %convolution_convert_fusion, bf16[]{:T(256)} %constant.37.clone.1), kind=kCustom, calls=%fused_computation.40 | custom fusion | bytes 4194816 | tf_op jit(solution)/shard_map/scatter | solution.py:28
  182.6 7.4 %reshape.136 = bf16[32,8,8192]{2,1,0:T(8,128)(2,1)} reshape(bf16[4096,512]{1,0:T(8,128)(2,1)} %scatter_custom_fusion.1) | data formatting | bytes 8388608 | tf_op jit(solution)/shard_map/reshape | solution.py:32
  208.7 87.6 %all-to-all-done.2 = bf16[32,8,8192]{2,1,0:T(8,128)(2,1)} async-done(((bf16[32,8,8192]{2,1,0:T(8,128)(2,1)}), bf16[32,8,8192]{2,1,0:T(8,128)(2,1)}, u32[]{:S(2)}, u32[]{:S(2)}) %all-to-all-start.2) | async-done | bytes 4194336 | tf_op jit(solution)/shard_map/all_to_all | solution.py:104
  296.3 7.0 %all-to-all-start.7 = ((bf16[32,8,2048]{2,0,1:T(8,128)(2,1)}), bf16[32,8,2048]{2,0,1:T(8,128)(2,1)S(1)}, u32[]{:S(2)}, u32[]{:S(2)}) async-start(bf16[32,8,2048]{2,0,1:T(8,128)(2,1)} %copy.58), calls=%async_computation.7 | async-start | bytes 2097152 | tf_op jit(solution)/shard_map/all_to_all | solution.py:110
  306.3 184.4 %all-reduce.3.cloned.1.call-done = (f32[512,512]{1,0:T(8,128)}, f32[128,512]{1,0:T(8,128)}, f32[32,512]{1,0:T(8,128)}) async-done(((f32[512,512]{1,0:T(8,128)}, f32[128,512]{1,0:T(8,128)}, f32[32,512]{1,0:T(8,128)}), (f32[512,512]{1,0:T(8,128)}, f32[128,512]{1,0:T(8,128)}, f32[32,512]{1,0:T(8,128)})) %all-reduce.3.cloned.1.call-update) | async-done | bytes 1376272 | tf_op jit(solution)/shard_map/psum | solution.py:160
  496.9 6.5 %copy.53 = bf16[32,8,8192]{2,0,1:T(8,128)(2,1)} copy(bf16[32,8,8192]{2,1,0:T(8,128)(2,1)} %all-to-all-done.2) | data formatting | bytes 8388608 | tf_op jit(solution)/shard_map/all_to_all | solution.py:104
  503.4 6.4 %all-to-all-start.3 = ((bf16[32,8,8192]{2,0,1:T(8,128)(2,1)}), bf16[32,8,8192]{2,0,1:T(8,128)(2,1)}, u32[]{:S(2)}, u32[]{:S(2)}) async-start(bf16[32,8,8192]{2,0,1:T(8,128)(2,1)} %copy.53), calls=%async_computation.3 | async-start | bytes 8388608 | tf_op jit(solution)/shard_map/all_to_all | solution.py:103
  509.8 23.5 %while.27 = (s32[]{:T(128)}, f32[8,32,512]{2,1,0:T(8,128)S(1)}, s32[32,8,16]{2,1,0:T(8,128)}, s32[8]{0:T(128)S(1)}, bf16[4096,32]{1,0:T(8,128)(2,1)S(1)}, /*index=5*/s32[4096]{0:T(1024)S(1)}, s32[]{:T(128)}) while((s32[]{:T(128)}, f32[8,32,512]{2,1,0:T(8,128)S(1)}, s32[32,8,16]{2,1,0:T(8,128)}, s32[8]{0:T(128)S(1)}, ...), condition=%wide.wide.region_18.19_spmd, body=%wide.wide.region_17.18_spmd.sunk | while | flops 136315392 | bytes 1134697 | solution.py:52
  535.3 13.0 %while.26 = (s32[]{:T(128)}, f32[4,512,128]{2,1,0:T(8,128)}, s32[4]{0:T(128)S(1)}, s32[32,8,16]{2,1,0:T(8,128)}, bf16[4096,128]{1,0:T(8,128)(2,1)S(1)}, /*index=5*/s32[4096]{0:T(1024)S(1)}, s32[]{:T(128)}) while((s32[]{:T(128)}, f32[4,512,128]{2,1,0:T(8,128)}, s32[4]{0:T(128)S(1)}, s32[32,8,16]{2,1,0:T(8,128)}, ...), condition=%wide.wide.region_11.12_spmd, body=%wide.wide.region_10.11_spmd.sunk | while | flops 538968576 | bytes 1331305 | solution.py:52
  548.3 10.2 %all-to-all-done.3 = bf16[32,8,8192]{2,0,1:T(8,128)(2,1)} async-done(((bf16[32,8,8192]{2,0,1:T(8,128)(2,1)}), bf16[32,8,8192]{2,0,1:T(8,128)(2,1)}, u32[]{:S(2)}, u32[]{:S(2)}) %all-to-all-start.3) | async-done | bytes 4194336 | tf_op jit(solution)/shard_map/all_to_all | solution.py:103
  558.6 6.5 %copy.54 = bf16[32,8,8192]{2,1,0:T(8,128)(2,1)} copy(bf16[32,8,8192]{2,0,1:T(8,128)(2,1)} %all-to-all-done.3) | data formatting | bytes 8388608 | tf_op jit(solution)/shard_map/all_to_all | solution.py:103
  565.0 7.4 %reshape.137 = bf16[4096,512]{1,0:T(8,128)(2,1)} reshape(bf16[32,8,8192]{2,1,0:T(8,128)(2,1)} %copy.54) | data formatting | bytes 8388608 | tf_op jit(solution)/shard_map/reshape | solution.py:146
  (180 shorter events, 135.5 us)
Async XLA Ops:
  7.2 159.2 %copy-start = (bf16[2048,512]{1,0:T(8,128)(2,1)S(1)}, bf16[2048,512]{1,0:T(8,128)(2,1)}, u32[]{:S(2)}) copy-start(bf16[2048,512]{1,0:T(8,128)(2,1)} %param.19) | copy-start | bytes 6291460
  12.9 22.6 %copy-start.12 = (s32[2048,1]{0,1:T(1,128)S(1)}, s32[2048,1]{0,1:T(1,128)}, u32[]{:S(2)}) copy-start(s32[2048,1]{0,1:T(1,128)} %param.29) | copy-start | bytes 24580
  23.5 32.8 %all-to-all-start = ((s32[32,1,128]{2,1,0:T(1,128)}), s32[32,1,128]{2,1,0:T(1,128)S(1)}, u32[]{:S(2)}, u32[]{:S(2)}) async-start(s32[32,1,128]{2,1,0:T(1,128)} %reshape.208), calls=%async_computation | async-start | bytes 32768 | tf_op jit(solution)/shard_map/all_to_all | solution.py:125
  46.3 62.2 %copy-start.18 = (bf16[32,512]{1,0:T(8,128)(2,1)S(1)}, bf16[32,512]{1,0:T(8,128)(2,1)}, u32[]{:S(2)}) copy-start(bf16[32,512]{1,0:T(8,128)(2,1)} %param.27) | copy-start | bytes 98308
  56.3 18.3 %all-to-all-start.4 = ((s32[32,1,128]{2,1,0:T(1,128)}), s32[32,1,128]{2,1,0:T(1,128)S(1)}, u32[]{:S(2)}, u32[]{:S(2)}) async-start(s32[32,1,128]{2,1,0:T(1,128)} %reshape.212), calls=%async_computation.4 | async-start | bytes 32768 | tf_op jit(solution)/shard_map/all_to_all | solution.py:132
  74.6 17.8 %all-to-all-start.8 = ((s32[32,1,128]{2,1,0:T(1,128)}), s32[32,1,128]{2,1,0:T(1,128)S(1)}, u32[]{:S(2)}, u32[]{:S(2)}) async-start(s32[32,1,128]{2,1,0:T(1,128)} %reshape.216), calls=%async_computation.8 | async-start | bytes 32768 | tf_op jit(solution)/shard_map/all_to_all | solution.py:139
  92.4 12.2 %all-to-all-start.1 = ((s32[8,1,512]{2,1,0:T(1,128)}), s32[8,1,512]{2,1,0:T(1,128)S(1)}, u32[]{:S(2)}, u32[]{:S(2)}) async-start(s32[8,1,512]{2,1,0:T(1,128)} %reshape.210), calls=%async_computation.1 | async-start | bytes 32768 | tf_op jit(solution)/shard_map/all_to_all | solution.py:124
  104.6 15.4 %all-to-all-start.5 = ((s32[8,1,512]{2,1,0:T(1,128)}), s32[8,1,512]{2,1,0:T(1,128)S(1)}, u32[]{:S(2)}, u32[]{:S(2)}) async-start(s32[8,1,512]{2,1,0:T(1,128)} %reshape.214), calls=%async_computation.5 | async-start | bytes 32768 | tf_op jit(solution)/shard_map/all_to_all | solution.py:131
  111.9 39.6 %copy-start.10 = (bf16[128,512]{1,0:T(8,128)(2,1)S(1)}, bf16[128,512]{1,0:T(8,128)(2,1)}, u32[]{:S(2)}) copy-start(bf16[128,512]{1,0:T(8,128)(2,1)} %param.26) | copy-start | bytes 393220
  120.0 26.9 %copy-start.14 = (s32[8,1,512]{2,1,0:T(1,128)}, s32[8,1,512]{2,1,0:T(1,128)S(1)}, u32[]{:S(2)}) copy-start(s32[8,1,512]{2,1,0:T(1,128)S(1)} %all-to-all-done.5) | copy-start | bytes 49156
  120.0 16.0 %all-to-all-start.10 = ((bf16[32,8,512]{2,1,0:T(8,128)(2,1)}), bf16[32,8,512]{2,1,0:T(8,128)(2,1)S(1)}, u32[]{:S(2)}, u32[]{:S(2)}) async-start(bf16[32,8,512]{2,1,0:T(8,128)(2,1)} %reshape.145), calls=%async_computation.10 | async-start | bytes 524288 | tf_op jit(solution)/shard_map/all_to_all | solution.py:118
  136.0 10.9 %all-to-all-start.9 = ((s32[8,1,512]{2,1,0:T(1,128)}), s32[8,1,512]{2,1,0:T(1,128)S(1)}, u32[]{:S(2)}, u32[]{:S(2)}) async-start(s32[8,1,512]{2,1,0:T(1,128)} %reshape.218), calls=%async_computation.9 | async-start | bytes 32768 | tf_op jit(solution)/shard_map/all_to_all | solution.py:138
  147.4 14.8 %all-to-all-start.11 = ((bf16[32,8,512]{2,0,1:T(8,128)(2,1)}), bf16[32,8,512]{2,0,1:T(8,128)(2,1)S(1)}, u32[]{:S(2)}, u32[]{:S(2)}) async-start(bf16[32,8,512]{2,0,1:T(8,128)(2,1)} %copy.65), calls=%async_computation.11 | async-start | bytes 524288 | tf_op jit(solution)/shard_map/all_to_all | solution.py:117
  162.2 32.2 %all-to-all-start.6 = ((bf16[32,8,2048]{2,1,0:T(8,128)(2,1)}), bf16[32,8,2048]{2,1,0:T(8,128)(2,1)S(1)}, u32[]{:S(2)}, u32[]{:S(2)}) async-start(bf16[32,8,2048]{2,1,0:T(8,128)(2,1)} %reshape.140), calls=%async_computation.6 | async-start | bytes 2097152 | tf_op jit(solution)/shard_map/all_to_all | solution.py:111
  190.0 9.8 %copy-start.9 = (bf16[32,2048]{1,0:T(8,128)(2,1)S(1)}, bf16[32,2048]{1,0:T(8,128)(2,1)}, u32[]{:S(2)}) copy-start(bf16[32,2048]{1,0:T(8,128)(2,1)} %param.24) | copy-start | bytes 393220
  194.4 101.9 %all-to-all-start.2 = ((bf16[32,8,8192]{2,1,0:T(8,128)(2,1)}), bf16[32,8,8192]{2,1,0:T(8,128)(2,1)}, u32[]{:S(2)}, u32[]{:S(2)}) async-start(bf16[32,8,8192]{2,1,0:T(8,128)(2,1)} %reshape.136), calls=%async_computation.2 | async-start | bytes 8388608 | tf_op jit(solution)/shard_map/all_to_all | solution.py:104
  199.7 291.0 %all-reduce.3.cloned.1.call-start = ((), (), s32[]{:S(2)}) async-start(), calls=%async_computation.12 | async-start | bytes 2752512 | tf_op jit(solution)/shard_map/psum | solution.py:160
  207.1 97.2 %copy-start.15 = (s32[8,1,512]{2,1,0:T(1,128)S(1)}, s32[8,1,512]{2,1,0:T(1,128)}, u32[]{:S(2)}) copy-start(s32[8,1,512]{2,1,0:T(1,128)} %copy-done.14) | copy-start | bytes 49156
  207.2 98.1 %copy-start.17 = (s32[8,1,512]{2,1,0:T(1,128)S(1)}, s32[8,1,512]{2,1,0:T(1,128)}, u32[]{:S(2)}) copy-start(s32[8,1,512]{2,1,0:T(1,128)} %copy-done.16) | copy-start | bytes 49156
  296.3 207.1 %all-to-all-start.7 = ((bf16[32,8,2048]{2,0,1:T(8,128)(2,1)}), bf16[32,8,2048]{2,0,1:T(8,128)(2,1)S(1)}, u32[]{:S(2)}, u32[]{:S(2)}) async-start(bf16[32,8,2048]{2,0,1:T(8,128)(2,1)} %copy.58), calls=%async_computation.7 | async-start | bytes 2097152 | tf_op jit(solution)/shard_map/all_to_all | solution.py:110
  305.2 191.7 %copy-start.6 = (s32[32,8,16]{2,1,0:T(8,128)}, s32[32,8,16]{2,1,0:T(8,128)S(1)}, u32[]{:S(2)}) copy-start(s32[32,8,16]{2,1,0:T(8,128)S(1)} %copy.60) | copy-start | bytes 49156
  306.2 190.7 %copy-start.7 = (s32[32,8,16]{2,1,0:T(8,128)}, s32[32,8,16]{2,1,0:T(8,128)S(1)}, u32[]{:S(2)}) copy-start(s32[32,8,16]{2,1,0:T(8,128)S(1)} %copy.67) | copy-start | bytes 49156
  503.4 6.4 %copy-start.8 = (f32[8,32,512]{2,1,0:T(8,128)S(1)}, f32[8,32,512]{2,1,0:T(8,128)}, u32[]{:S(2)}) copy-start(f32[8,32,512]{2,1,0:T(8,128)} %custom-call.1) | copy-start | bytes 1572868
  503.4 55.2 %all-to-all-start.3 = ((bf16[32,8,8192]{2,0,1:T(8,128)(2,1)}), bf16[32,8,8192]{2,0,1:T(8,128)(2,1)}, u32[]{:S(2)}, u32[]{:S(2)}) async-start(bf16[32,8,8192]{2,0,1:T(8,128)(2,1)} %copy.53), calls=%async_computation.3 | async-start | bytes 8388608 | tf_op jit(solution)/shard_map/all_to_all | solution.py:103
  (11 other events, 26.9 us)
Sparse Core Ops, SparseCore 0:
  207.3 283.4 all-reduce.2
where the time goes:
time: 595 us; the launch traced here: 585 us
  waiting for transfers between devices  311 us (52%)
  local copies, waits for them, and re-layouts  110 us (18%)
  starting transfers between devices  78.9 us (13%)
  matrix products  43.6 us (7%)
  other arithmetic  26.6 us (4%)
  between operations  14.9 us (3%)
    psum x1, waiting for transfers between devices, per_device(): lax.psum((part_hot, part_warm, part_cold), ('wide', 'narrow'))  184 us
    all_to_all x1, waiting for transfers between devices, per_device(): lax.all_to_all(sent_hot, 'wide', split_axis=0, concat_axis=0, tiled=True)  87.6 us
    scatter x3, local copies, waits for them, and re-layouts, pack_rows(): jnp.zeros((devices * capacity, columns), values.dtype).at[placed]  25.4 us
    scatter x3, local copies, waits for them, and re-layouts, pack_rows(): jnp.full((devices * capacity,), -1, jnp.int32).at[placed].set(local_rows)  24.7 us
    dot_general x5, matrix products, one_block(): return jnp.dot(onehot, terms, preferred_element_type=jnp.float32)  13.7 us
    dot_general x8, matrix products, one_block(): lax.dot_general(terms, onehot, (((0,), (0,)), ((), ())), preferred_elemen...  13.6 us
    all_to_all x1, starting transfers between devices, per_device(): lax.all_to_all(label_hot, 'wide', split_axis=0, concat_axis=0, tiled=True)  12 us
  transfers between devices with their start and end apart: 13, of which 8 were waited for; matrix products, arithmetic and copies ran while one was open for 24% of the time, Pallas kernels for 0%

commit v1 on v0

--- a/solution.py
+++ b/solution.py
@@ -158,7 +158,7 @@
     part_cold = jnp.dot(saved_cold, upstream_cold, preferred_element_type=jnp.float32)
     factor = 1.0 / math.sqrt(LOOK * devices)
     total_hot, total_warm, total_cold = lax.psum(
-        (part_hot, part_warm, part_cold), ("wide", "narrow")
+        lax.psum((part_hot, part_warm, part_cold), "wide"), "narrow"
     )
     return (
         table_hot,

time: 595 us -> 523 us (0.88)
  waiting for transfers between devices: 311 us -> 233 us
    psum x1 -> x2, waiting for transfers between devices: 184 us -> 112 us  [the longest x1 69.9 us: per_device(): lax.psum((part_hot, part_warm, part_cold), 'wide')]
    all_to_all x1, waiting for transfers between devices: 10.2 us -> 0.01 us  [per_device(): lax.all_to_all(lax.all_to_all(sent_hot, 'wide', split_axis=0, concat_axis...]
  transfers between devices with their start and end apart: 13 -> 14, of which waited for: 8 -> 8; matrix products, arithmetic and copies ran while one was open for 24% -> 28% of each run, Pallas kernels for 0% -> 0%
where the time goes in v1:
time: 523 us; the launch traced here: 513 us
  waiting for transfers between devices  233 us (45%)
  local copies, waits for them, and re-layouts  110 us (21%)
  starting transfers between devices  84.7 us (16%)
  matrix products  43.6 us (8%)
  other arithmetic  26.1 us (5%)
  between operations  14.9 us (3%)
    all_to_all x1, waiting for transfers between devices, per_device(): lax.all_to_all(sent_hot, 'wide', split_axis=0, concat_axis=0, tiled=True)  92.3 us
    psum x1, waiting for transfers between devices, per_device(): lax.psum((part_hot, part_warm, part_cold), 'wide')  69.9 us
    psum x1, waiting for transfers between devices, per_device(): lax.psum(lax.psum((part_hot, part_warm, part_cold), 'wide'), 'narrow')  42 us
    scatter x3, local copies, waits for them, and re-layouts, pack_rows(): jnp.zeros((devices * capacity, columns), values.dtype).at[placed]  25.4 us
    scatter x3, local copies, waits for them, and re-layouts, pack_rows(): jnp.full((devices * capacity,), -1, jnp.int32).at[placed].set(local_rows)  24.7 us
    dot_general x5, matrix products, one_block(): return jnp.dot(onehot, terms, preferred_element_type=jnp.float32)  13.7 us
    dot_general x8, matrix products, one_block(): lax.dot_general(terms, onehot, (((0,), (0,)), ((), ())), preferred_elemen...  13.6 us
    all_to_all x1, starting transfers between devices, per_device(): lax.all_to_all(label_hot, 'wide', split_axis=0, concat_axis=0, tiled=True)  12 us
  transfers between devices with their start and end apart: 14, of which 8 were waited for; matrix products, arithmetic and copies ran while one was open for 28% of the time, Pallas kernels for 0%

profile of v1, /device:TPU:1, one launch (start us, length us, event | category | flops | bytes accessed | tf_op | source)
XLA Modules:
  0.0 512.7 jit_solution(8167377467799768238)
XLA Ops:
  14.5 8.2 %scatter_custom_fusion = s32[4096]{0:T(1024)S(1)} fusion(s32[2048]{0:T(1024)S(1)} %bitcast.108, s32[2048]{0:T(1024)} %param.31, s32[]{:T(128)} %constant.28.clone.1), kind=kCustom, calls=%fused_computation.69 | custom fusion | bytes 16896 | tf_op jit(solution)/shard_map/scatter | solution.py:29
  23.5 12.0 %all-to-all-start = ((s32[32,1,128]{2,1,0:T(1,128)}), s32[32,1,128]{2,1,0:T(1,128)S(1)}, u32[]{:S(2)}, u32[]{:S(2)}) async-start(s32[32,1,128]{2,1,0:T(1,128)} %reshape.208), calls=%async_computation | async-start | bytes 32768 | tf_op jit(solution)/shard_map/all_to_all | solution.py:125
  47.3 8.2 %scatter_custom_fusion.2 = s32[4096]{0:T(1024)S(1)} fusion(s32[2048]{0:T(1024)S(1)} %bitcast.110, s32[2048]{0:T(1024)} %param.32, s32[]{:T(128)} %constant.28.clone.1), kind=kCustom, calls=%fused_computation.67 | custom fusion | bytes 16896 | tf_op jit(solution)/shard_map/scatter | solution.py:29
  56.3 9.2 %all-to-all-start.4 = ((s32[32,1,128]{2,1,0:T(1,128)}), s32[32,1,128]{2,1,0:T(1,128)S(1)}, u32[]{:S(2)}, u32[]{:S(2)}) async-start(s32[32,1,128]{2,1,0:T(1,128)} %reshape.212), calls=%async_computation.4 | async-start | bytes 32768 | tf_op jit(solution)/shard_map/all_to_all | solution.py:132
  65.6 8.2 %scatter_custom_fusion.4 = s32[4096]{0:T(1024)S(1)} fusion(s32[2048]{0:T(1024)S(1)} %bitcast.112, s32[2048]{0:T(1024)} %param.33, s32[]{:T(128)} %constant.28.clone.1), kind=kCustom, calls=%fused_computation.65 | custom fusion | bytes 16896 | tf_op jit(solution)/shard_map/scatter | solution.py:29
  74.6 9.2 %all-to-all-start.8 = ((s32[32,1,128]{2,1,0:T(1,128)}), s32[32,1,128]{2,1,0:T(1,128)S(1)}, u32[]{:S(2)}, u32[]{:S(2)}) async-start(s32[32,1,128]{2,1,0:T(1,128)} %reshape.216), calls=%async_computation.8 | async-start | bytes 32768 | tf_op jit(solution)/shard_map/all_to_all | solution.py:139
  85.9 6.5 %all-to-all-done.8 = s32[32,1,128]{2,1,0:T(1,128)S(1)} async-done(((s32[32,1,128]{2,1,0:T(1,128)}), s32[32,1,128]{2,1,0:T(1,128)S(1)}, u32[]{:S(2)}, u32[]{:S(2)}) %all-to-all-start.8) | async-done | bytes 16416 | tf_op jit(solution)/shard_map/all_to_all | solution.py:139
  92.4 7.5 %all-to-all-start.1 = ((s32[8,1,512]{2,1,0:T(1,128)}), s32[8,1,512]{2,1,0:T(1,128)S(1)}, u32[]{:S(2)}, u32[]{:S(2)}) async-start(s32[8,1,512]{2,1,0:T(1,128)} %reshape.210), calls=%async_computation.1 | async-start | bytes 32768 | tf_op jit(solution)/shard_map/all_to_all | solution.py:124
  111.9 6.4 %scatter_custom_fusion.5 = bf16[4096,32]{1,0:T(8,128)(2,1)S(1)} fusion(s32[2048]{0:T(1024)S(1)} %bitcast.113, bf16[2048,32]{1,0:T(8,128)(2,1)} %copy.64, bf16[]{:T(256)} %constant.37.clone.1), kind=kCustom, calls=%fused_computation.53 | custom fusion | bytes 262656 | tf_op jit(solution)/shard_map/scatter | solution.py:28
  125.4 10.6 %all-to-all-done.10 = bf16[32,8,512]{2,1,0:T(8,128)(2,1)S(1)} async-done(((bf16[32,8,512]{2,1,0:T(8,128)(2,1)}), bf16[32,8,512]{2,1,0:T(8,128)(2,1)S(1)}, u32[]{:S(2)}, u32[]{:S(2)}) %all-to-all-start.10) | async-done | bytes 262176 | tf_op jit(solution)/shard_map/all_to_all | solution.py:118
  136.0 6.2 %all-to-all-start.9 = ((s32[8,1,512]{2,1,0:T(1,128)}), s32[8,1,512]{2,1,0:T(1,128)S(1)}, u32[]{:S(2)}, u32[]{:S(2)}) async-start(s32[8,1,512]{2,1,0:T(1,128)} %reshape.218), calls=%async_computation.9 | async-start | bytes 32768 | tf_op jit(solution)/shard_map/all_to_all | solution.py:138
  154.6 6.4 %scatter_custom_fusion.3 = bf16[4096,128]{1,0:T(8,128)(2,1)S(1)} fusion(s32[2048]{0:T(1024)} %bitcast.111, bf16[2048,128]{1,0:T(8,128)(2,1)} %convolution_convert_fusion.1, bf16[]{:T(256)} %constant.37.clone.1), kind=kCustom, calls=%fused_computation.55 | custom fusion | bytes 1049088 | tf_op jit(solution)/shard_map/scatter | solution.py:28
  170.0 12.6 %scatter_custom_fusion.1 = bf16[4096,512]{1,0:T(8,128)(2,1)} fusion(s32[2048]{0:T(1024)} %bitcast.109, bf16[2048,512]{1,0:T(8,128)(2,1)} %convolution_convert_fusion, bf16[]{:T(256)} %constant.37.clone.1), kind=kCustom, calls=%fused_computation.40 | custom fusion | bytes 4194816 | tf_op jit(solution)/shard_map/scatter | solution.py:28
  182.6 7.4 %reshape.136 = bf16[32,8,8192]{2,1,0:T(8,128)(2,1)} reshape(bf16[4096,512]{1,0:T(8,128)(2,1)} %scatter_custom_fusion.1) | data formatting | bytes 8388608 | tf_op jit(solution)/shard_map/reshape | solution.py:32
  208.7 92.3 %all-to-all-done.2 = bf16[32,8,8192]{2,1,0:T(8,128)(2,1)} async-done(((bf16[32,8,8192]{2,1,0:T(8,128)(2,1)}), bf16[32,8,8192]{2,1,0:T(8,128)(2,1)}, u32[]{:S(2)}, u32[]{:S(2)}) %all-to-all-start.2) | async-done | bytes 4194336 | tf_op jit(solution)/shard_map/all_to_all | solution.py:104
  301.0 9.0 %all-to-all-start.7 = ((bf16[32,8,2048]{2,0,1:T(8,128)(2,1)}), bf16[32,8,2048]{2,0,1:T(8,128)(2,1)S(1)}, u32[]{:S(2)}, u32[]{:S(2)}) async-start(bf16[32,8,2048]{2,0,1:T(8,128)(2,1)} %copy.58), calls=%async_computation.7 | async-start | bytes 2097152 | tf_op jit(solution)/shard_map/all_to_all | solution.py:110
  313.6 69.9 %all-reduce.5.cloned.1.call-done = (f32[512,512]{1,0:T(8,128)}, f32[128,512]{1,0:T(8,128)}, f32[32,512]{1,0:T(8,128)}) async-done(((f32[512,512]{1,0:T(8,128)}, f32[128,512]{1,0:T(8,128)}, f32[32,512]{1,0:T(8,128)}), (f32[512,512]{1,0:T(8,128)}, f32[128,512]{1,0:T(8,128)}, f32[32,512]{1,0:T(8,128)})) %all-reduce.5.cloned.1.call-update) | async-done | bytes 1376272 | tf_op jit(solution)/shard_map/psum | solution.py:161
  383.5 6.5 %copy.53 = bf16[32,8,8192]{2,0,1:T(8,128)(2,1)} copy(bf16[32,8,8192]{2,1,0:T(8,128)(2,1)} %all-to-all-done.2) | data formatting | bytes 8388608 | tf_op jit(solution)/shard_map/all_to_all | solution.py:104
  390.0 10.2 %all-to-all-start.3 = ((bf16[32,8,8192]{2,0,1:T(8,128)(2,1)}), bf16[32,8,8192]{2,0,1:T(8,128)(2,1)}, u32[]{:S(2)}, u32[]{:S(2)}) async-start(bf16[32,8,8192]{2,0,1:T(8,128)(2,1)} %copy.53), calls=%async_computation.3 | async-start | bytes 8388608 | tf_op jit(solution)/shard_map/all_to_all | solution.py:103
  400.1 23.5 %while.27 = (s32[]{:T(128)}, f32[8,32,512]{2,1,0:T(8,128)S(1)}, s32[32,8,16]{2,1,0:T(8,128)}, s32[8]{0:T(128)S(1)}, bf16[4096,32]{1,0:T(8,128)(2,1)S(1)}, /*index=5*/s32[4096]{0:T(1024)S(1)}, s32[]{:T(128)}) while((s32[]{:T(128)}, f32[8,32,512]{2,1,0:T(8,128)S(1)}, s32[32,8,16]{2,1,0:T(8,128)}, s32[8]{0:T(128)S(1)}, ...), condition=%wide.wide.region_18.19_spmd, body=%wide.wide.region_17.18_spmd.sunk | while | flops 136315392 | bytes 1134697 | solution.py:52
  424.5 42.0 %all-reduce.7.cloned.1.call-done = (f32[512,512]{1,0:T(8,128)}, f32[128,512]{1,0:T(8,128)}, f32[32,512]{1,0:T(8,128)}) async-done(((f32[512,512]{1,0:T(8,128)}, f32[128,512]{1,0:T(8,128)}, f32[32,512]{1,0:T(8,128)}), (f32[512,512]{1,0:T(8,128)}, f32[128,512]{1,0:T(8,128)}, f32[32,512]{1,0:T(8,128)})) %all-reduce.7.cloned.1.call-update) | async-done | bytes 1376272 | tf_op jit(solution)/shard_map/psum | solution.py:160
  473.1 13.0 %while.26 = (s32[]{:T(128)}, f32[4,512,128]{2,1,0:T(8,128)}, s32[4]{0:T(128)S(1)}, s32[32,8,16]{2,1,0:T(8,128)}, bf16[4096,128]{1,0:T(8,128)(2,1)S(1)}, /*index=5*/s32[4096]{0:T(1024)S(1)}, s32[]{:T(128)}) while((s32[]{:T(128)}, f32[4,512,128]{2,1,0:T(8,128)}, s32[4]{0:T(128)S(1)}, s32[32,8,16]{2,1,0:T(8,128)}, ...), condition=%wide.wide.region_11.12_spmd, body=%wide.wide.region_10.11_spmd.sunk | while | flops 538968576 | bytes 1331305 | solution.py:52
  486.1 6.5 %copy.54 = bf16[32,8,8192]{2,1,0:T(8,128)(2,1)} copy(bf16[32,8,8192]{2,0,1:T(8,128)(2,1)} %all-to-all-done.3) | data formatting | bytes 8388608 | tf_op jit(solution)/shard_map/all_to_all | solution.py:103
  492.5 7.4 %reshape.137 = bf16[4096,512]{1,0:T(8,128)(2,1)} reshape(bf16[32,8,8192]{2,1,0:T(8,128)(2,1)} %copy.54) | data formatting | bytes 8388608 | tf_op jit(solution)/shard_map/reshape | solution.py:146
  (181 shorter events, 135.2 us)
Async XLA Ops:
  7.2 159.2 %copy-start = (bf16[2048,512]{1,0:T(8,128)(2,1)S(1)}, bf16[2048,512]{1,0:T(8,128)(2,1)}, u32[]{:S(2)}) copy-start(bf16[2048,512]{1,0:T(8,128)(2,1)} %param.19) | copy-start | bytes 6291460
  12.9 22.6 %copy-start.11 = (s32[2048,1]{0,1:T(1,128)S(1)}, s32[2048,1]{0,1:T(1,128)}, u32[]{:S(2)}) copy-start(s32[2048,1]{0,1:T(1,128)} %param.29) | copy-start | bytes 24580
  23.5 32.8 %all-to-all-start = ((s32[32,1,128]{2,1,0:T(1,128)}), s32[32,1,128]{2,1,0:T(1,128)S(1)}, u32[]{:S(2)}, u32[]{:S(2)}) async-start(s32[32,1,128]{2,1,0:T(1,128)} %reshape.208), calls=%async_computation | async-start | bytes 32768 | tf_op jit(solution)/shard_map/all_to_all | solution.py:125
  46.3 62.2 %copy-start.17 = (bf16[32,512]{1,0:T(8,128)(2,1)S(1)}, bf16[32,512]{1,0:T(8,128)(2,1)}, u32[]{:S(2)}) copy-start(bf16[32,512]{1,0:T(8,128)(2,1)} %param.27) | copy-start | bytes 98308
  56.3 18.3 %all-to-all-start.4 = ((s32[32,1,128]{2,1,0:T(1,128)}), s32[32,1,128]{2,1,0:T(1,128)S(1)}, u32[]{:S(2)}, u32[]{:S(2)}) async-start(s32[32,1,128]{2,1,0:T(1,128)} %reshape.212), calls=%async_computation.4 | async-start | bytes 32768 | tf_op jit(solution)/shard_map/all_to_all | solution.py:132
  74.6 17.8 %all-to-all-start.8 = ((s32[32,1,128]{2,1,0:T(1,128)}), s32[32,1,128]{2,1,0:T(1,128)S(1)}, u32[]{:S(2)}, u32[]{:S(2)}) async-start(s32[32,1,128]{2,1,0:T(1,128)} %reshape.216), calls=%async_computation.8 | async-start | bytes 32768 | tf_op jit(solution)/shard_map/all_to_all | solution.py:139
  92.4 12.2 %all-to-all-start.1 = ((s32[8,1,512]{2,1,0:T(1,128)}), s32[8,1,512]{2,1,0:T(1,128)S(1)}, u32[]{:S(2)}, u32[]{:S(2)}) async-start(s32[8,1,512]{2,1,0:T(1,128)} %reshape.210), calls=%async_computation.1 | async-start | bytes 32768 | tf_op jit(solution)/shard_map/all_to_all | solution.py:124
  104.6 15.4 %all-to-all-start.5 = ((s32[8,1,512]{2,1,0:T(1,128)}), s32[8,1,512]{2,1,0:T(1,128)S(1)}, u32[]{:S(2)}, u32[]{:S(2)}) async-start(s32[8,1,512]{2,1,0:T(1,128)} %reshape.214), calls=%async_computation.5 | async-start | bytes 32768 | tf_op jit(solution)/shard_map/all_to_all | solution.py:131
  111.9 39.6 %copy-start.9 = (bf16[128,512]{1,0:T(8,128)(2,1)S(1)}, bf16[128,512]{1,0:T(8,128)(2,1)}, u32[]{:S(2)}) copy-start(bf16[128,512]{1,0:T(8,128)(2,1)} %param.26) | copy-start | bytes 393220
  120.0 26.9 %copy-start.13 = (s32[8,1,512]{2,1,0:T(1,128)}, s32[8,1,512]{2,1,0:T(1,128)S(1)}, u32[]{:S(2)}) copy-start(s32[8,1,512]{2,1,0:T(1,128)S(1)} %all-to-all-done.5) | copy-start | bytes 49156
  120.0 16.0 %all-to-all-start.10 = ((bf16[32,8,512]{2,1,0:T(8,128)(2,1)}), bf16[32,8,512]{2,1,0:T(8,128)(2,1)S(1)}, u32[]{:S(2)}, u32[]{:S(2)}) async-start(bf16[32,8,512]{2,1,0:T(8,128)(2,1)} %reshape.145), calls=%async_computation.10 | async-start | bytes 524288 | tf_op jit(solution)/shard_map/all_to_all | solution.py:118
  136.0 10.9 %all-to-all-start.9 = ((s32[8,1,512]{2,1,0:T(1,128)}), s32[8,1,512]{2,1,0:T(1,128)S(1)}, u32[]{:S(2)}, u32[]{:S(2)}) async-start(s32[8,1,512]{2,1,0:T(1,128)} %reshape.218), calls=%async_computation.9 | async-start | bytes 32768 | tf_op jit(solution)/shard_map/all_to_all | solution.py:138
  147.4 14.8 %all-to-all-start.11 = ((bf16[32,8,512]{2,0,1:T(8,128)(2,1)}), bf16[32,8,512]{2,0,1:T(8,128)(2,1)S(1)}, u32[]{:S(2)}, u32[]{:S(2)}) async-start(bf16[32,8,512]{2,0,1:T(8,128)(2,1)} %copy.65), calls=%async_computation.11 | async-start | bytes 524288 | tf_op jit(solution)/shard_map/all_to_all | solution.py:117
  162.3 32.2 %all-to-all-start.6 = ((bf16[32,8,2048]{2,1,0:T(8,128)(2,1)}), bf16[32,8,2048]{2,1,0:T(8,128)(2,1)S(1)}, u32[]{:S(2)}, u32[]{:S(2)}) async-start(bf16[32,8,2048]{2,1,0:T(8,128)(2,1)} %reshape.140), calls=%async_computation.6 | async-start | bytes 2097152 | tf_op jit(solution)/shard_map/all_to_all | solution.py:111
  190.0 9.8 %copy-start.8 = (bf16[32,2048]{1,0:T(8,128)(2,1)S(1)}, bf16[32,2048]{1,0:T(8,128)(2,1)}, u32[]{:S(2)}) copy-start(bf16[32,2048]{1,0:T(8,128)(2,1)} %param.24) | copy-start | bytes 393220
  194.4 106.6 %all-to-all-start.2 = ((bf16[32,8,8192]{2,1,0:T(8,128)(2,1)}), bf16[32,8,8192]{2,1,0:T(8,128)(2,1)}, u32[]{:S(2)}, u32[]{:S(2)}) async-start(bf16[32,8,8192]{2,1,0:T(8,128)(2,1)} %reshape.136), calls=%async_computation.2 | async-start | bytes 8388608 | tf_op jit(solution)/shard_map/all_to_all | solution.py:104
  199.7 183.8 %all-reduce.5.cloned.1.call-start = ((), (), s32[]{:S(2)}) async-start(), calls=%async_computation.12 | async-start | bytes 2752512 | tf_op jit(solution)/shard_map/psum | solution.py:161
  207.1 103.9 %copy-start.14 = (s32[8,1,512]{2,1,0:T(1,128)S(1)}, s32[8,1,512]{2,1,0:T(1,128)}, u32[]{:S(2)}) copy-start(s32[8,1,512]{2,1,0:T(1,128)} %copy-done.13) | copy-start | bytes 49156
  207.1 104.8 %copy-start.16 = (s32[8,1,512]{2,1,0:T(1,128)S(1)}, s32[8,1,512]{2,1,0:T(1,128)}, u32[]{:S(2)}) copy-start(s32[8,1,512]{2,1,0:T(1,128)} %copy-done.15) | copy-start | bytes 49156
  301.0 89.0 %all-to-all-start.7 = ((bf16[32,8,2048]{2,0,1:T(8,128)(2,1)}), bf16[32,8,2048]{2,0,1:T(8,128)(2,1)S(1)}, u32[]{:S(2)}, u32[]{:S(2)}) async-start(bf16[32,8,2048]{2,0,1:T(8,128)(2,1)} %copy.58), calls=%async_computation.7 | async-start | bytes 2097152 | tf_op jit(solution)/shard_map/all_to_all | solution.py:110
  310.1 156.4 %all-reduce.7.cloned.1.call-start = ((), (), s32[]{:S(2)}) async-start(), calls=%async_computation.13 | async-start | bytes 2752512 | tf_op jit(solution)/shard_map/psum | solution.py:160
  311.8 78.2 %copy-start.6 = (s32[32,8,16]{2,1,0:T(8,128)}, s32[32,8,16]{2,1,0:T(8,128)S(1)}, u32[]{:S(2)}) copy-start(s32[32,8,16]{2,1,0:T(8,128)S(1)} %copy.60) | copy-start | bytes 49156
  312.7 77.2 %copy-start.7 = (s32[32,8,16]{2,1,0:T(8,128)}, s32[32,8,16]{2,1,0:T(8,128)S(1)}, u32[]{:S(2)}) copy-start(s32[32,8,16]{2,1,0:T(8,128)S(1)} %copy.67) | copy-start | bytes 49156
  390.0 96.1 %all-to-all-start.3 = ((bf16[32,8,8192]{2,0,1:T(8,128)(2,1)}), bf16[32,8,8192]{2,0,1:T(8,128)(2,1)}, u32[]{:S(2)}, u32[]{:S(2)}) async-start(bf16[32,8,8192]{2,0,1:T(8,128)(2,1)} %copy.53), calls=%async_computation.3 | async-start | bytes 8388608 | tf_op jit(solution)/shard_map/all_to_all | solution.py:103
  (11 other events, 26.9 us)
Sparse Core Ops, SparseCore 0:
  207.3 176.1 all-reduce.4
  386.0 80.4 all-reduce.6
